TPU v7x, 512 devices: a whole 4x4x16 slice. The times are simulated.
512 devices in a mesh: replica: 8 (over z_lo), shard: 64 (over z_hi, x, y, core).
Axes of the slice: x: 4, y: 4, z: 16 (z_hi: 2, z_lo: 8; z = z_hi * 8 + z_lo), core: 2. Of those that a mesh axis runs over, the one named last changes fastest.
Arguments:
- pseudo_grads: bfloat16 [8, 2, 5120, 5120], P('replica', None, 'shard'), may hold values from -400 to 400
- momentum: float32 [2, 5120, 5120], P(None, 'shard', 'replica'), may hold values from -3 to 3
Outputs:
- update: bfloat16 [2, 5120, 5120], P(None, 'shard')
- momentum_next: float32 [2, 5120, 5120], P(None, 'shard', 'replica')
All inputs are finite; a program needn't handle non-finite values.
Results may differ from a plain program's by a relative error of at most 0.015.
Values may be sent and summed in bfloat16 or wider, within the bound.
A program may use at most 64 MiB of HBM per device.

v0:
```python
import math

import jax
import jax.numpy as jnp
from jax import lax
from jax.sharding import PartitionSpec as P

HD = 5120
ITERS = 5
BLOCK = 80


QUINTIC_FIRST = 3.4445
QUINTIC_SECOND = -4.775
QUINTIC_THIRD = 2.0315
MOMENTUM_RATE = 0.9
EPSILON = 1e-07
EXACTNESS = lax.Precision.HIGHEST


def from_everyone(value, axis):
    copies = jnp.broadcast_to(value, (lax.axis_size(axis), *value.shape))
    return lax.all_to_all(copies, axis, split_axis=0, concat_axis=0, tiled=True)


def of_everyone(value, axis):
    everything = from_everyone(value, axis)
    return jnp.sum(everything, axis=0)


def split_up(value, dim, devices):
    lengths = value.shape
    parts = value.reshape(*lengths[:dim], devices, lengths[dim] // devices, *lengths[dim + 1 :])
    return jnp.moveaxis(parts, dim, 0)


def summed_on_arrival(value, axis, dim):
    parts = split_up(value, dim, lax.axis_size(axis))
    arrived = lax.all_to_all(parts, axis, split_axis=0, concat_axis=0, tiled=True)
    return arrived.astype(jnp.float32).sum(axis=0)


def block_view(matrix):
    layer_count, row_count, col_count = matrix.shape
    return matrix.reshape(layer_count, row_count // BLOCK, BLOCK, col_count)


def gram_local(blocks):
    return jnp.einsum("lbik,lbjk->lbij", blocks, blocks, precision=EXACTNESS)


def polish(blocks, gram_matrix):
    mixture = QUINTIC_SECOND * gram_matrix + QUINTIC_THIRD * jnp.einsum(
        "lbij,lbjk->lbik", gram_matrix, gram_matrix, precision=EXACTNESS
    )
    return QUINTIC_FIRST * blocks + jnp.einsum(
        "lbij,lbjk->lbik", mixture, blocks, precision=EXACTNESS
    )


def shard_norm(squares):
    return of_everyone(squares, "shard")


def body(pseudo_grads, momentum):
    replicas = lax.axis_size("replica")
    terms = pseudo_grads.astype(jnp.float32)
    summed = summed_on_arrival(terms.astype(jnp.bfloat16), "replica", 3)[0]
    average = summed / replicas
    momentum_next = MOMENTUM_RATE * momentum + average
    direction = average + MOMENTUM_RATE * momentum_next
    gathered = lax.all_gather(direction.astype(jnp.bfloat16), "replica", axis=2, tiled=True).astype(
        direction.dtype
    )
    blocks = block_view(gathered)
    raw_gram = gram_local(blocks)
    traces = jnp.sum(jnp.trace(raw_gram, axis1=2, axis2=3), axis=1)
    squares = shard_norm(traces)
    factor = 1.0 / (jnp.sqrt(squares) + EPSILON)
    blocks = blocks * factor[:, None, None, None]
    gram_matrix = raw_gram * (factor * factor)[:, None, None, None]
    for iteration in range(ITERS):
        if iteration > 0:
            gram_matrix = gram_local(blocks)
        blocks = polish(blocks, gram_matrix)
    layer_count, block_count, block_rows, col_count = blocks.shape
    finished = (
        (blocks * math.sqrt(HD))
        .reshape(layer_count, block_count * block_rows, col_count)
        .astype(jnp.bfloat16)
    )
    return (finished, momentum_next)


def solution(mesh):
    placed = (P("replica", None, "shard", None), P(None, "shard", "replica"))
    return jax.shard_map(
        body,
        mesh=mesh,
        in_specs=placed,
        out_specs=(P(None, "shard", None), P(None, "shard", "replica")),
        check_vma=False,
    )
```

profile of v0, /device:TPU:1, one launch (start us, length us, event | category | flops | bytes accessed | tf_op | source)
XLA Modules:
  0.0 235.9 jit_solution(9793180782383251182)
XLA Ops:
  7.2 0.0 all-gather.2.cloned.1.call-start
  7.2 1.7 copy.9
  8.9 0.2 copy.6
  9.1 0.0 copy-start.1
  9.1 88.4 %all_to_all.11 = bf16[8,1,2,80,640]{4,3,2,1,0:T(8,128)(2,1)S(1)} all-to-all(bf16[8,1,2,80,640]{4,3,2,1,0:T(8,128)(2,1)S(1)} %copy.6), channel_id=1, replica_groups=mesh['replica'=8,'shard'=64] {'replica'}, dimensions={0} | all-to-all | bytes 3276800 | tf_op jit(solution)/shard_map/all_to_all | solution.py:39
  97.5 0.2 convert_reduce_fusion
  97.8 0.0 copy-done.1
  97.8 0.9 add_convert_fusion
  98.7 0.0 all-gather.2.cloned.1.call-update
  98.7 61.3 %all-gather.2.cloned.1.call-done = bf16[2,80,5120]{2,1,0:T(8,128)(2,1)} async-done(((bf16[2,80,640]{2,1,0:T(8,128)(2,1)}), bf16[2,80,5120]{2,1,0:T(8,128)(2,1)}) %all-gather.2.cloned.1.call-update) | async-done | bytes 1638416 | tf_op jit(solution)/shard_map/all_gather | solution.py:72
  160.0 0.0 copy-start
  160.0 2.7 %select_reduce_fusion = (f32[2]{0:T(128)S(1)}, f32[2,80,80]{2,1,0:T(8,128)S(1)}) fusion(pred[80,80]{1,0:T(8,128)(4,1)S(1)} %iota_compare_fusion, bf16[2,80,5120]{2,1,0:T(8,128)(2,1)} %all-gather.2.cloned.1.call-done), kind=kOutput, calls=%fused_computation.24 | convolution fusion | flops 131097600 | bytes 1696008 | tf_op jit(solution)/shard_map/lbik,lbjk->lbij/dot_general | solution.py:49
  162.8 34.9 %all_to_all.12 = f32[64,1,2]{2,1,0:T(1,128)S(1)} all-to-all(f32[64,1,2]{2,1,0:T(1,128)S(1)} %broadcast_in_dim.16), channel_id=1, replica_groups=mesh['replica'=8,'shard'=64] {'shard'}, dimensions={0} | all-to-all | bytes 1024 | tf_op jit(solution)/shard_map/all_to_all | solution.py:23
  197.6 0.1 reduce_sum.34
  197.7 0.3 fusion.9
  198.0 0.0 copy-done
  198.1 3.2 %convolution_add_fusion.4 = f32[2,80,5120]{2,1,0:T(8,128)S(1)} fusion(f32[2,80,80]{2,1,0:T(8,128)S(1)} %fusion.9, bf16[2,80,5120]{2,1,0:T(8,128)(2,1)S(1)} %copy-done, f32[2]{0:T(128)S(1)} %get-tuple-element.3), kind=kOutput, calls=%fused_computation.4 | convolution fusion | flops 791347200 | bytes 4966408 | tf_op jit(solution)/shard_map/lbij,lbjk->lbik/dot_general | solution.py:56
  201.3 3.2 %fusion.13 = f32[2,80,80]{2,1,0:T(8,128)S(1)} fusion(f32[2,80,5120]{2,1,0:T(8,128)S(1)} %convolution_add_fusion.4), kind=kOutput, calls=%fused_computation.29 | convolution fusion | flops 786432000 | bytes 3328000 | tf_op jit(solution)/shard_map/lbik,lbjk->lbij/dot_general | solution.py:49
  204.4 0.2 fusion.8
  204.7 3.2 %convolution_add_fusion.3 = f32[2,80,5120]{2,1,0:T(8,128)S(1)} fusion(f32[2,80,80]{2,1,0:T(8,128)S(1)} %fusion.8, f32[2,80,5120]{2,1,0:T(8,128)S(1)} %convolution_add_fusion.4), kind=kOutput, calls=%fused_computation.3 | convolution fusion | flops 788070400 | bytes 6604800 | tf_op jit(solution)/shard_map/lbij,lbjk->lbik/dot_general | solution.py:56
  207.8 3.4 %fusion.14 = f32[2,80,80]{2,1,0:T(8,128)S(1)} fusion(f32[2,80,5120]{2,1,0:T(8,128)S(1)} %convolution_add_fusion.3), kind=kOutput, calls=%fused_computation.30 | convolution fusion | flops 786432000 | bytes 3328000 | tf_op jit(solution)/shard_map/lbik,lbjk->lbij/dot_general | solution.py:49
  211.3 0.2 fusion.7
  211.5 3.2 %convolution_add_fusion.2 = f32[2,80,5120]{2,1,0:T(8,128)S(1)} fusion(f32[2,80,80]{2,1,0:T(8,128)S(1)} %fusion.7, f32[2,80,5120]{2,1,0:T(8,128)S(1)} %convolution_add_fusion.3), kind=kOutput, calls=%fused_computation.2 | convolution fusion | flops 788070400 | bytes 6604800 | tf_op jit(solution)/shard_map/lbij,lbjk->lbik/dot_general | solution.py:56
  214.6 3.2 %fusion.15 = f32[2,80,80]{2,1,0:T(8,128)S(1)} fusion(f32[2,80,5120]{2,1,0:T(8,128)S(1)} %convolution_add_fusion.2), kind=kOutput, calls=%fused_computation.31 | convolution fusion | flops 786432000 | bytes 3328000 | tf_op jit(solution)/shard_map/lbik,lbjk->lbij/dot_general | solution.py:49
  217.8 0.2 fusion.6
  218.0 3.2 %convolution_add_fusion.1 = f32[2,80,5120]{2,1,0:T(8,128)S(1)} fusion(f32[2,80,80]{2,1,0:T(8,128)S(1)} %fusion.6, f32[2,80,5120]{2,1,0:T(8,128)S(1)} %convolution_add_fusion.2), kind=kOutput, calls=%fused_computation.1 | convolution fusion | flops 788070400 | bytes 6604800 | tf_op jit(solution)/shard_map/lbij,lbjk->lbik/dot_general | solution.py:56
  221.2 3.5 %fusion.16 = f32[2,80,80]{2,1,0:T(8,128)S(1)} fusion(f32[2,80,5120]{2,1,0:T(8,128)S(1)} %convolution_add_fusion.1), kind=kOutput, calls=%fused_computation.32 | convolution fusion | flops 786432000 | bytes 3328000 | tf_op jit(solution)/shard_map/lbik,lbjk->lbij/dot_general | solution.py:49
  224.7 0.2 fusion.5
  224.9 4.2 %fusion.1 = bf16[2,80,5120]{2,1,0:T(8,128)(2,1)} fusion(f32[2,80,80]{2,1,0:T(8,128)S(1)} %fusion.5, f32[2,80,5120]{2,1,0:T(8,128)S(1)} %convolution_add_fusion.1), kind=kOutput, calls=%fused_computation.6 | convolution fusion | flops 789708800 | bytes 4966400 | tf_op jit(solution)/shard_map/lbij,lbjk->lbik/dot_general | solution.py:56
  (3 shorter events, 0.0 us)
Async XLA Ops:
  7.2 152.8 %all-gather.2.cloned.1.call-start = ((), (), s32[]{:S(2)}) async-start(), calls=%async_computation.2 | async-start | bytes 1843200 | tf_op jit(solution)/shard_map/all_gather | solution.py:72
  9.1 88.6 %copy-start.1 = (f32[2,80,640]{2,1,0:T(8,128)S(1)}, f32[2,80,640]{2,1,0:T(8,128)}, u32[]{:S(2)}) copy-start(f32[2,80,640]{2,1,0:T(8,128)} %param.3) | copy-start | bytes 1228804
  160.0 38.0 %copy-start = (bf16[2,80,5120]{2,1,0:T(8,128)(2,1)S(1)}, bf16[2,80,5120]{2,1,0:T(8,128)(2,1)}, u32[]{:S(2)}) copy-start(bf16[2,80,5120]{2,1,0:T(8,128)(2,1)} %all-gather.2.cloned.1.call-done) | copy-start | bytes 4915204
Sparse Core Ops, SparseCore 0:
  98.8 61.1 all-gather.1
where the time goes:
time: 236 us
  blocking collectives  123 us (52%)
  waiting for transfers between devices  61.3 us (26%)
  matrix products  33.9 us (14%)
  between operations  14.2 us (6%)
    all_to_all x1, blocking collectives, summed_on_arrival(): lax.all_to_all(parts, axis, split_axis=0, concat_axis=0, tiled=True)  88.4 us
    all_gather x1, waiting for transfers between devices, body(): lax.all_gather(direction.astype(jnp.bfloat16), 'replica', axis=2, tiled=T...  61.3 us
    all_to_all x1, blocking collectives, from_everyone(): return lax.all_to_all(copies, axis, split_axis=0, concat_axis=0, tiled=True)  34.9 us
    dot_general x5, matrix products, polish(): jnp.einsum('lbij,lbjk->lbik', mixture, blocks, precision=EXACTNESS)  16.8 us
    dot_general x5, matrix products, gram_local(): return jnp.einsum('lbik,lbjk->lbij', blocks, blocks, precision=EXACTNESS)  15.9 us
  transfers between devices with their start and end apart: 1, of which 1 were waited for; matrix products, arithmetic and copies ran while one was open for 0% of the time, Pallas kernels for 0%

commit v1 on v0

v1 whole, which is shorter than its diff:
```python
import functools
import math

import jax
import jax.numpy as jnp
from jax import lax
from jax.experimental import pallas as pl
from jax.experimental.pallas import tpu as pltpu
from jax.sharding import PartitionSpec as P

ITERS = 5
QUINTIC_FIRST = 3.4445
QUINTIC_SECOND = -4.775
QUINTIC_THIRD = 2.0315
MOMENTUM_RATE = 0.9
EPSILON = 1e-07
EXACTNESS = lax.Precision.HIGHEST
MESH = pl.DeviceIdType.MESH

SHARD_AXES = (2, 4, 4, 2)
TILE = 128
LAG = 5


def kernel(
    n, axes, grads_hbm, moment_hbm, out_hbm, next_hbm,
    grads, moment, fresh, gathered, right_part, left_part, gram, squares, plane_in, ring_in, result,
    load_sem, right_recv, left_recv, gather_recv, right_send, left_send, gather_right, gather_left,
    plane_send, plane_recv, ring_send, ring_recv, token_up, token_down, store_sem,
):
    halves, xs, ys, cores = axes
    layers, rows, cols = grads.shape
    width = cols // n
    per_layer = width // TILE
    slices = layers * per_layer
    last = n - 1
    ring = halves * n

    i = lax.axis_index("replica")
    shard = lax.axis_index("shard")
    core = lax.rem(shard, cores)
    y = lax.rem(lax.div(shard, cores), ys)
    x = lax.rem(lax.div(shard, cores * ys), xs)
    half = lax.div(shard, cores * ys * xs)
    z = half * n + i
    in_plane = shard - half * (cores * ys * xs)

    def along_z(offset):
        there = lax.rem(z + offset, ring)
        return (lax.rem(there, n), lax.div(there, n) * (cores * ys * xs) + in_plane)

    def along_x(offset):
        there = lax.rem(x + offset, xs)
        return (i, ((half * xs + there) * ys + y) * cores + core)

    def along_y(offset):
        there = lax.rem(y + offset, ys)
        return (i, ((half * xs + x) * ys + there) * cores + core)

    def along_core(offset):
        there = lax.rem(core + offset, cores)
        return (i, ((half * xs + x) * ys + y) * cores + there)

    stages = [(along_x, xs), (along_y, ys), (along_core, cores)]
    stages = [s for s in stages if s[1] > 1]
    right, left = (i + 1, shard), (i - 1, shard)
    up, down = along_z(1), along_z(ring - 1)

    loads = [
        pltpu.make_async_copy(grads_hbm.at[0], grads, load_sem.at[0]),
        pltpu.make_async_copy(moment_hbm, moment, load_sem.at[1]),
    ]
    for load in loads:
        load.start()

    barrier = pltpu.get_barrier_semaphore()
    friends = [up, down]
    for where, size in stages:
        friends += [where(offset) for offset in range(1, size)]
    for friend in friends:
        pl.semaphore_signal(barrier, inc=1, device_id=friend, device_id_type=MESH)

    gram[...] = jnp.zeros_like(gram)
    squares[...] = jnp.zeros_like(squares)
    for s in range(slices):
        right_part[s, 0] = jnp.zeros((rows, TILE), jnp.bfloat16)
        left_part[s, last] = jnp.zeros((rows, TILE), jnp.bfloat16)
    for load in loads:
        load.wait()
    pl.semaphore_wait(barrier, len(friends))

    def columns(s, j):
        return pl.ds(pl.multiple_of(j * width + lax.rem(s, per_layer) * TILE, TILE), TILE)

    def layer(s):
        return lax.div(s, per_layer)

    def part_copy(part, s, j, send, recv, target):
        return pltpu.make_async_remote_copy(
            src_ref=part.at[s, j], dst_ref=part.at[s, j], send_sem=send.at[s, j], recv_sem=recv.at[s, j],
            device_id=target, device_id_type=MESH)

    def chunk_copy(s, c, send, target):
        chunk = gathered.at[layer(s), :, columns(s, c)]
        return pltpu.make_async_remote_copy(
            src_ref=chunk, dst_ref=chunk, send_sem=send.at[s, c], recv_sem=gather_recv.at[s, c],
            device_id=target, device_id_type=MESH)

    def hop(part, s, j, send, recv, target, first):
        own = grads.at[layer(s), :, columns(s, j)]

        @pl.when(i == first)
        def _():
            pltpu.make_async_remote_copy(
                src_ref=own, dst_ref=part.at[s, j], send_sem=send.at[s, j], recv_sem=recv.at[s, j],
                device_id=target, device_id_type=MESH).start()

        @pl.when(i != first)
        def _():
            copy = part_copy(part, s, j, send, recv, target)
            copy.wait_recv()
            total = part[s, j].astype(jnp.float32) + own[...].astype(jnp.float32)
            part[s, j] = total.astype(jnp.bfloat16)
            copy.start()

    upper = lax.div(i, n // 2)
    far = upper * i + (1 - upper) * (last - i)
    final_at = last - far + far * LAG
    closing = (slices - 1) * last + final_at

    def finish(s):
        @pl.when(i > 0)
        def _():
            part_copy(right_part, s, i, right_send, right_recv, right).wait_recv()

        @pl.when(i < last)
        def _():
            part_copy(left_part, s, i, left_send, left_recv, left).wait_recv()

        k = layer(s)
        here = pl.ds(pl.multiple_of(lax.rem(s, per_layer) * TILE, TILE), TILE)
        total = (
            grads[k, :, columns(s, i)].astype(jnp.float32)
            + right_part[s, i].astype(jnp.float32)
            + left_part[s, i].astype(jnp.float32)
        )
        average = total / n
        moment_next = MOMENTUM_RATE * moment[k, :, here] + average
        direction = average + MOMENTUM_RATE * moment_next
        fresh[k, :, here] = moment_next
        gathered[k, :, columns(s, i)] = direction.astype(jnp.bfloat16)
        row_sum = jnp.sum(direction * direction, axis=0, keepdims=True)
        squares[0, pl.ds(k, 1), :] += row_sum

        @pl.when(i < last)
        def _():
            chunk_copy(s, i, gather_right, right).start()

        @pl.when(i > 0)
        def _():
            chunk_copy(s, i, gather_left, left).start()

    def exchange(stage):
        where, size = stages[stage]
        return [
            pltpu.make_async_remote_copy(
                src_ref=squares.at[stage], dst_ref=plane_in.at[stage, offset], send_sem=plane_send.at[stage, offset],
                recv_sem=plane_recv.at[stage, offset], device_id=where(offset), device_id_type=MESH)
            for offset in range(1, size)
        ]

    def add_up(stage):
        total = squares[stage]
        for offset, copy in enumerate(exchange(stage), 1):
            copy.wait_recv()
            total = total + plane_in[stage, offset]
        squares[stage + 1] = total

    def around(offset):
        return pltpu.make_async_remote_copy(
            src_ref=squares.at[len(stages)], dst_ref=ring_in.at[offset], send_sem=ring_send.at[offset],
            recv_sem=ring_recv.at[offset], device_id=along_z(offset), device_id_type=MESH)

    def tick(t, carry):
        @pl.when((lax.rem(t, 4) == 0) & (t < 2 * ring))
        def _():
            pl.semaphore_signal(token_up, inc=1, device_id=up, device_id_type=MESH)
            pl.semaphore_signal(token_down, inc=1, device_id=down, device_id_type=MESH)
            pl.semaphore_wait(token_up, 1)
            pl.semaphore_wait(token_down, 1)

        to_right = t - i * LAG
        @pl.when((to_right >= 0) & (to_right < last * slices))
        def _():
            s, j = lax.div(to_right, last), last - lax.rem(to_right, last)
            @pl.when(i < j)
            def _():
                hop(right_part, s, j, right_send, right_recv, right, 0)

        to_left = t - (last - i) * LAG
        @pl.when((to_left >= 0) & (to_left < last * slices))
        def _():
            s, j = lax.div(to_left, last), lax.rem(to_left, last)
            @pl.when(i > j)
            def _():
                hop(left_part, s, j, left_send, left_recv, left, last)

        since = t - final_at
        @pl.when((since >= 0) & (since < last * slices))
        def _():
            @pl.when(lax.rem(since, last) == 0)
            def _():
                finish(lax.div(since, last))

        @pl.when(t == closing)
        def _():
            pltpu.make_async_copy(fresh, next_hbm, store_sem.at[0]).start()
            if stages:
                for copy in exchange(0):
                    copy.start()

        for stage in range(len(stages)):
            @pl.when(t == closing + 5 * (stage + 1))
            def _():
                add_up(stage)
                if stage + 1 < len(stages):
                    for copy in exchange(stage + 1):
                        copy.start()

        @pl.when(t == closing + 5 * len(stages))
        def _():
            for offset in range(1, ring):
                around(offset).start()

        for c in reversed(range(last)):
            if c >= n // 2:
                due = last - c + i * LAG
            else:
                due = c + (last + i - 2 * c) * LAG
            late = t - due
            @pl.when((c < i) & (late >= 0) & (late < last * slices))
            def _():
                @pl.when(lax.rem(late, last) == 0)
                def _():
                    copy = chunk_copy(lax.div(late, last), c, gather_right, right)
                    copy.wait_recv()
                    @pl.when(i < last)
                    def _():
                        copy.start()

        for back in reversed(range(last)):
            c = last - back
            if back >= n // 2:
                due = last - back + (last - i) * LAG
            else:
                due = back + (last + last - i - 2 * back) * LAG
            late = t - due
            @pl.when((c > i) & (late >= 0) & (late < last * slices))
            def _():
                @pl.when(lax.rem(late, last) == 0)
                def _():
                    copy = chunk_copy(lax.div(late, last), c, gather_left, left)
                    copy.wait_recv()
                    @pl.when(i > 0)
                    def _():
                        copy.start()

        whole = t - (last + far) * LAG - 1
        @pl.when((whole >= 0) & (whole < last * slices))
        def _():
            @pl.when(lax.rem(whole, last) == 0)
            def _():
                s = lax.div(whole, last)
                k = layer(s)
                band = jnp.concatenate([gathered[k, :, columns(s, c)] for c in range(n)], axis=1)
                gram[k] += lax.dot_general(
                    band, band, (((1,), (1,)), ((), ())), preferred_element_type=jnp.float32)

        return carry

    ticks = (slices - 1) * last + 2 * last * LAG + 2
    lax.fori_loop(0, ticks, tick, 0)

    total = squares[len(stages)]
    for offset in range(1, ring):
        around(offset).wait_recv()
        total = total + ring_in[offset]

    eye = (lax.broadcasted_iota(jnp.int32, (rows, rows), 0) == lax.broadcasted_iota(jnp.int32, (rows, rows), 1))
    eye = eye.astype(jnp.float32)
    product = functools.partial(jnp.dot, precision=EXACTNESS, preferred_element_type=jnp.float32)
    factors, states, mixes = [], [], []
    for k in range(layers):
        norm = jnp.sqrt(jnp.sum(total[k : k + 1, :], axis=1, keepdims=True))
        factor = 1.0 / (norm + EPSILON)
        factors.append(factor)
        states.append(gram[k] * (factor * factor))
        mixes.append(None)
    for step in range(ITERS):
        for k in range(layers):
            state = states[k]
            square = product(state, state)
            poly = QUINTIC_FIRST * eye + QUINTIC_SECOND * state + QUINTIC_THIRD * square
            mixes[k] = poly if mixes[k] is None else product(poly, mixes[k])
            if step + 1 < ITERS:
                states[k] = product(product(state, poly), poly)

    span = cols // 4
    for k in range(layers):
        mix = mixes[k] * (factors[k] * math.sqrt(cols))
        high = mix.astype(jnp.bfloat16)
        low = (mix - high.astype(jnp.float32)).astype(jnp.bfloat16)
        for at in range(cols // span):
            window = pl.ds(at * span, span)
            block = gathered[k, :, window]
            value = jnp.dot(high, block, preferred_element_type=jnp.float32)
            value = value + jnp.dot(low, block, preferred_element_type=jnp.float32)
            result[k, :, window] = value.astype(jnp.bfloat16)
            pltpu.make_async_copy(
                result.at[k, :, window], out_hbm.at[k, :, window], store_sem.at[1 + k * (cols // span) + at]).start()

    def drain(s, carry):
        for j in range(n):
            if j > 0:
                @pl.when(i < j)
                def _():
                    part_copy(right_part, s, j, right_send, right_recv, right).wait_send()
            if j < last:
                @pl.when(i > j)
                def _():
                    part_copy(left_part, s, j, left_send, left_recv, left).wait_send()
            @pl.when((i < last) & (j <= i))
            def _():
                chunk_copy(s, j, gather_right, right).wait_send()
            @pl.when((i > 0) & (j >= i))
            def _():
                chunk_copy(s, j, gather_left, left).wait_send()
        return carry

    lax.fori_loop(0, slices, drain, 0)
    for stage in range(len(stages)):
        for copy in exchange(stage):
            copy.wait_send()
    for offset in range(1, ring):
        around(offset).wait_send()
    pltpu.make_async_copy(fresh, next_hbm, store_sem.at[0]).wait()
    for k in range(layers):
        for at in range(cols // span):
            window = pl.ds(at * span, span)
            pltpu.make_async_copy(
                result.at[k, :, window], out_hbm.at[k, :, window], store_sem.at[1 + k * (cols // span) + at]).wait()


def body(axes, pseudo_grads, momentum):
    n = lax.axis_size("replica")
    _, layers, rows, cols = pseudo_grads.shape
    width = cols // n
    slices = layers * width // TILE
    ring = axes[0] * n
    dma = pltpu.SemaphoreType.DMA
    any_spec = pl.BlockSpec(memory_space=pl.ANY)
    bf16, f32 = jnp.bfloat16, jnp.float32
    return pl.pallas_call(
        functools.partial(kernel, n, axes),
        out_shape=(
            jax.ShapeDtypeStruct((layers, rows, cols), bf16),
            jax.ShapeDtypeStruct((layers, rows, width), f32),
        ),
        in_specs=[any_spec, any_spec],
        out_specs=(any_spec, any_spec),
        scratch_shapes=[
            pltpu.VMEM((layers, rows, cols), bf16),
            pltpu.VMEM((layers, rows, width), f32),
            pltpu.VMEM((layers, rows, width), f32),
            pltpu.VMEM((layers, rows, cols), bf16),
            pltpu.VMEM((slices, n, rows, TILE), bf16),
            pltpu.VMEM((slices, n, rows, TILE), bf16),
            pltpu.VMEM((layers, rows, rows), f32),
            pltpu.VMEM((4, 8, TILE), f32),
            pltpu.VMEM((3, 4, 8, TILE), f32),
            pltpu.VMEM((ring, 8, TILE), f32),
            pltpu.VMEM((layers, rows, cols), bf16),
            dma((2,)),
            dma((slices, n)),
            dma((slices, n)),
            dma((slices, n)),
            dma((slices, n)),
            dma((slices, n)),
            dma((slices, n)),
            dma((slices, n)),
            dma((3, 4)),
            dma((3, 4)),
            dma((ring,)),
            dma((ring,)),
            pltpu.SemaphoreType.REGULAR,
            pltpu.SemaphoreType.REGULAR,
            dma((16,)),
        ],
        compiler_params=pltpu.CompilerParams(
            collective_id=0, has_side_effects=True, vmem_limit_bytes=40 * 1024 * 1024),
    )(pseudo_grads, momentum)


def solution(mesh, axes=SHARD_AXES):
    placed = (P("replica", None, "shard", None), P(None, "shard", "replica"))
    return jax.shard_map(
        functools.partial(body, axes),
        mesh=mesh,
        in_specs=placed,
        out_specs=(P(None, "shard", None), P(None, "shard", "replica")),
        check_vma=False,
    )
```

time: 236 us -> 118 us (0.50)
  the two profiles are of different devices: /device:TPU:1 before, /device:TPU:2 now
where the time goes in v1:
time: 118 us; the launch traced here: 117 us
  Pallas kernels  112 us (95%)
  local copies, waits for them, and re-layouts  4.34 us (4%)
    pallas_call x1, Pallas kernels, body(): pl.pallas_call(functools.partial(kernel, n, axes), out_shape=(jax.ShapeDt...  112 us
    unnamed x6, local copies, waits for them, and re-layouts  4.34 us

profile of v1, /device:TPU:2, one launch (start us, length us, event | category | flops | bytes accessed | tf_op | source)
XLA Modules:
  0.0 117.5 jit_solution(12123774131979669743)
XLA Ops:
  0.6 0.0 copy-start
  0.6 1.4 %copy-done = bf16[1,2,80,5120]{3,2,1,0:T(8,128)(2,1)S(1)} copy-done((bf16[1,2,80,5120]{3,2,1,0:T(8,128)(2,1)S(1)}, bf16[1,2,80,5120]{3,2,1,0:T(8,128)(2,1)}, u32[]{:S(2)}) %copy-start) | copy-done | bytes 1638424
  2.1 0.0 copy-start.1
  2.1 1.0 copy-done.1
  3.1 112.5 %shard_map.41 = (bf16[2,80,5120]{2,1,0:T(8,128)(2,1)S(1)}, f32[2,80,640]{2,1,0:T(8,128)S(1)}) custom-call(bf16[1,2,80,5120]{3,2,1,0:T(8,128)(2,1)S(1)} %copy-done, f32[2,80,640]{2,1,0:T(8,128)S(1)} %copy-done.1), custom_call_target="tpu_custom_call" | custom-call | tf_op jit(solution)/shard_map/pallas_call | solution.py:363
  115.5 1.2 copy.6
  116.7 0.8 copy.7
Async XLA Ops:
  0.6 1.4 %copy-start = (bf16[1,2,80,5120]{3,2,1,0:T(8,128)(2,1)S(1)}, bf16[1,2,80,5120]{3,2,1,0:T(8,128)(2,1)}, u32[]{:S(2)}) copy-start(bf16[1,2,80,5120]{3,2,1,0:T(8,128)(2,1)} %grads_hbm.1) | copy-start | bytes 4915204
  2.1 1.0 copy-start.1

commit v2 on v0

v2 whole, which is shorter than its diff:
```python
import functools
import math

import jax
import jax.numpy as jnp
from jax import lax
from jax.experimental import pallas as pl
from jax.experimental.pallas import tpu as pltpu
from jax.sharding import PartitionSpec as P

ITERS = 5
QUINTIC_FIRST = 3.4445
QUINTIC_SECOND = -4.775
QUINTIC_THIRD = 2.0315
MOMENTUM_RATE = 0.9
EPSILON = 1e-07
EXACTNESS = lax.Precision.HIGHEST
MESH = pl.DeviceIdType.MESH

SHARD_AXES = (2, 4, 4, 2)
TILE = 128
GROUP = 8
LAG = 9


def kernel(
    n, axes, grads_hbm, moment_hbm, out_hbm, next_hbm,
    grads, moment, fresh, gathered, inward_part, cross_part, gram, squares, plane_in, ring_in, result,
    load_sem, inward_recv, cross_recv, outward_recv, inward_send, outward_send,
    plane_send, plane_recv, ring_send, ring_recv, store_sem,
):
    halves, xs, ys, cores = axes
    layers, rows, cols = grads.shape
    width = cols // n
    per_layer = cols // TILE
    messages = layers * per_layer
    ring = halves * n
    middle = n // 2 - 1

    gain = (1.0 + MOMENTUM_RATE) / n
    mixed = MOMENTUM_RATE * MOMENTUM_RATE / gain

    i = lax.axis_index("replica")
    shard = lax.axis_index("shard")
    core = lax.rem(shard, cores)
    y = lax.rem(lax.div(shard, cores), ys)
    x = lax.rem(lax.div(shard, cores * ys), xs)
    half = lax.div(shard, cores * ys * xs)
    z = half * n + i
    in_plane = shard - half * (cores * ys * xs)
    upper = lax.div(i, n // 2)
    depth = i + upper * (n - 1 - 2 * i)
    inward = (i + 1 - 2 * upper, shard)
    outward = (i - 1 + 2 * upper, shard)

    def along_z(offset):
        there = lax.rem(z + offset, ring)
        return (lax.rem(there, n), lax.div(there, n) * (cores * ys * xs) + in_plane)

    offsets = [(a, b, c) for a in range(xs) for b in range(ys) for c in range(cores)][1:]

    def across(a, b, c):
        there = (lax.rem(x + a, xs) * ys + lax.rem(y + b, ys)) * cores + lax.rem(core + c, cores)
        return (i, half * (cores * ys * xs) + there)

    up, down = along_z(1), along_z(ring - 1)

    loads = [
        pltpu.make_async_copy(moment_hbm, moment, load_sem.at[0]),
        pltpu.make_async_copy(grads_hbm.at[0], grads, load_sem.at[1]),
    ]
    for load in loads:
        load.start()

    barrier = pltpu.get_barrier_semaphore()
    for friend in (up, down):
        pl.semaphore_signal(barrier, inc=1, device_id=friend, device_id_type=MESH)

    if halves > 1:
        far = (n // 2 - upper, lax.rem(half + 1, halves) * (cores * ys * xs) + in_plane)
        pl.semaphore_signal(barrier, inc=1, device_id=far, device_id_type=MESH)

    @pl.when(depth == middle)
    def _():
        for offset in offsets:
            pl.semaphore_signal(barrier, inc=1, device_id=across(*offset), device_id_type=MESH)

    gram[...] = jnp.zeros_like(gram)
    squares[...] = jnp.zeros_like(squares)
    for load in loads:
        load.wait()
    mine = pl.ds(pl.multiple_of(i * width, TILE), width)
    for k in range(layers):
        own = grads[k, :, mine].astype(jnp.float32) + mixed * moment[k]
        grads[k, :, mine] = own.astype(jnp.bfloat16)

    @pl.when(depth == middle)
    def _():
        pl.semaphore_wait(barrier, 2 + len(offsets) + (halves - 1) * (n // 2))

    @pl.when(depth != middle)
    def _():
        pl.semaphore_wait(barrier, 2)

    def place(ref, m):
        column = pl.multiple_of(lax.rem(m, per_layer) * TILE, TILE)
        return ref.at[lax.div(m, per_layer), :, pl.ds(column, TILE)]

    def inward_copy(m, source):
        return pltpu.make_async_remote_copy(
            src_ref=source, dst_ref=inward_part.at[m], send_sem=inward_send.at[m], recv_sem=inward_recv.at[m],
            device_id=inward, device_id_type=MESH)

    def cross_copy(m):
        return pltpu.make_async_remote_copy(
            src_ref=inward_part.at[m], dst_ref=cross_part.at[m], send_sem=inward_send.at[m],
            recv_sem=cross_recv.at[m], device_id=inward, device_id_type=MESH)

    def outward_copy(m):
        chunk = place(gathered, m)
        return pltpu.make_async_remote_copy(
            src_ref=chunk, dst_ref=chunk, send_sem=outward_send.at[m], recv_sem=outward_recv.at[m],
            device_id=outward, device_id_type=MESH)

    def send_inward(m):
        own = place(grads, m)

        @pl.when(depth == 0)
        def _():
            inward_copy(m, own).start()

        @pl.when(depth > 0)
        def _():
            inward_copy(m, own).wait_recv()
            total = inward_part[m].astype(jnp.float32) + own[...].astype(jnp.float32)
            inward_part[m] = total.astype(jnp.bfloat16)

            @pl.when(depth < middle)
            def _():
                inward_copy(m, inward_part.at[m]).start()

            @pl.when(depth == middle)
            def _():
                cross_copy(m).start()

    def send_outward(m):
        @pl.when(depth == middle)
        def _():
            cross_copy(m).wait_recv()
            total = inward_part[m].astype(jnp.float32) + cross_part[m].astype(jnp.float32)
            place(gathered, m)[...] = total.astype(jnp.bfloat16)
            outward_copy(m).start()
            squares[0, pl.ds(lax.div(m, per_layer), 1), :] += jnp.sum(total * total, axis=0, keepdims=True)

        @pl.when(depth < middle)
        def _():
            outward_copy(m).wait_recv()

            @pl.when(depth > 0)
            def _():
                outward_copy(m).start()

        @pl.when(lax.rem(m, GROUP) == GROUP - 1)
        def _():
            k = lax.div(m, per_layer)
            first = pl.multiple_of((lax.rem(m, per_layer) - (GROUP - 1)) * TILE, TILE)
            band = gathered[k, :, pl.ds(first, GROUP * TILE)]
            gram[k] += lax.dot_general(band, band, (((1,), (1,)), ((), ())), preferred_element_type=jnp.float32)

    wait_for = (2 * middle + 1 - 2 * depth) * LAG

    def step(t, carry):
        @pl.when(t < messages)
        def _():
            send_inward(t)

        @pl.when(t >= wait_for)
        def _():
            send_outward(t - wait_for)

        return carry

    lax.fori_loop(0, messages + wait_for, step, 0)

    def plane_copies():
        return [
            pltpu.make_async_remote_copy(
                src_ref=squares.at[0], dst_ref=plane_in.at[at], send_sem=plane_send.at[at],
                recv_sem=plane_recv.at[at], device_id=across(*offset), device_id_type=MESH)
            for at, offset in enumerate(offsets)
        ]

    reach = ring // 2

    def ring_copy(offset):
        return pltpu.make_async_remote_copy(
            src_ref=squares.at[1], dst_ref=ring_in.at[half], send_sem=ring_send.at[offset],
            recv_sem=ring_recv.at[half], device_id=along_z(lax.rem(ring + (2 * upper - 1) * offset, ring)),
            device_id_type=MESH)

    def ring_arrival(source):
        return pltpu.make_async_remote_copy(
            src_ref=squares.at[1], dst_ref=ring_in.at[source], send_sem=ring_send.at[0],
            recv_sem=ring_recv.at[source], device_id=up, device_id_type=MESH)

    @pl.when(depth == middle)
    def _():
        copies = plane_copies()
        for copy in copies:
            copy.start()
        total = squares[0]
        for at, copy in enumerate(copies):
            copy.wait_recv()
            total = total + plane_in[at]
        squares[1] = total
        for offset in range(1, reach):
            ring_copy(offset).start()

    for k in range(layers):
        average = (gathered[k, :, mine].astype(jnp.float32) - mixed * moment[k]) / n
        fresh[k] = MOMENTUM_RATE * moment[k] + average
    pltpu.make_async_copy(fresh, next_hbm, store_sem.at[0]).start()

    for source in range(halves):
        @pl.when((depth == middle) & (half == source))
        def _():
            ring_in[source] = squares[1]

        @pl.when((depth != middle) | (half != source))
        def _():
            ring_arrival(source).wait_recv()

    total = ring_in[0]
    for source in range(1, halves):
        total = total + ring_in[source]

    eye = (lax.broadcasted_iota(jnp.int32, (rows, rows), 0) == lax.broadcasted_iota(jnp.int32, (rows, rows), 1))
    eye = eye.astype(jnp.float32)
    product = functools.partial(jnp.dot, precision=EXACTNESS, preferred_element_type=jnp.float32)
    factors, states, mixes = [], [], []
    for k in range(layers):
        norm = gain * jnp.sqrt(jnp.sum(total[k : k + 1, :], axis=1, keepdims=True))
        factor = gain / (norm + EPSILON)
        factors.append(factor)
        states.append(gram[k] * (factor * factor))
        mixes.append(None)
    for iteration in range(ITERS):
        for k in range(layers):
            state = states[k]
            square = product(state, state)
            poly = QUINTIC_FIRST * eye + QUINTIC_SECOND * state + QUINTIC_THIRD * square
            mixes[k] = poly if mixes[k] is None else product(poly, mixes[k])
            if iteration + 1 < ITERS:
                states[k] = product(product(state, poly), poly)

    span = cols // 4
    for k in range(layers):
        mix = mixes[k] * (factors[k] * math.sqrt(cols))
        high = mix.astype(jnp.bfloat16)
        low = (mix - high.astype(jnp.float32)).astype(jnp.bfloat16)
        for at in range(cols // span):
            window = pl.ds(at * span, span)
            block = gathered[k, :, window]
            value = jnp.dot(high, block, preferred_element_type=jnp.float32)
            value = value + jnp.dot(low, block, preferred_element_type=jnp.float32)
            result[k, :, window] = value.astype(jnp.bfloat16)
            pltpu.make_async_copy(
                result.at[k, :, window], out_hbm.at[k, :, window], store_sem.at[1 + k * (cols // span) + at]).start()

    def drain(m, carry):
        inward_copy(m, inward_part.at[m]).wait_send()

        @pl.when(depth > 0)
        def _():
            outward_copy(m).wait_send()

        return carry

    lax.fori_loop(0, messages, drain, 0)

    @pl.when(depth == middle)
    def _():
        for copy in plane_copies():
            copy.wait_send()
        for offset in range(1, reach):
            ring_copy(offset).wait_send()

    pltpu.make_async_copy(fresh, next_hbm, store_sem.at[0]).wait()
    for k in range(layers):
        for at in range(cols // span):
            window = pl.ds(at * span, span)
            pltpu.make_async_copy(
                result.at[k, :, window], out_hbm.at[k, :, window], store_sem.at[1 + k * (cols // span) + at]).wait()


def body(axes, pseudo_grads, momentum):
    n = lax.axis_size("replica")
    _, layers, rows, cols = pseudo_grads.shape
    width = cols // n
    messages = layers * cols // TILE
    ring = axes[0] * n
    plane = max(axes[1] * axes[2] * axes[3] - 1, 1)
    dma = pltpu.SemaphoreType.DMA
    any_spec = pl.BlockSpec(memory_space=pl.ANY)
    bf16, f32 = jnp.bfloat16, jnp.float32
    return pl.pallas_call(
        functools.partial(kernel, n, axes),
        out_shape=(
            jax.ShapeDtypeStruct((layers, rows, cols), bf16),
            jax.ShapeDtypeStruct((layers, rows, width), f32),
        ),
        in_specs=[any_spec, any_spec],
        out_specs=(any_spec, any_spec),
        scratch_shapes=[
            pltpu.VMEM((layers, rows, cols), bf16),
            pltpu.VMEM((layers, rows, width), f32),
            pltpu.VMEM((layers, rows, width), f32),
            pltpu.VMEM((layers, rows, cols), bf16),
            pltpu.VMEM((messages, rows, TILE), bf16),
            pltpu.VMEM((messages, rows, TILE), bf16),
            pltpu.VMEM((layers, rows, rows), f32),
            pltpu.VMEM((2, 8, TILE), f32),
            pltpu.VMEM((plane, 8, TILE), f32),
            pltpu.VMEM((axes[0], 8, TILE), f32),
            pltpu.VMEM((layers, rows, cols), bf16),
            dma((2,)),
            dma((messages,)),
            dma((messages,)),
            dma((messages,)),
            dma((messages,)),
            dma((messages,)),
            dma((plane,)),
            dma((plane,)),
            dma((ring,)),
            dma((axes[0],)),
            dma((16,)),
        ],
        compiler_params=pltpu.CompilerParams(
            collective_id=0, has_side_effects=True, vmem_limit_bytes=40 * 1024 * 1024),
    )(pseudo_grads, momentum)


def solution(mesh, axes=SHARD_AXES):
    placed = (P("replica", None, "shard", None), P(None, "shard", "replica"))
    return jax.shard_map(
        functools.partial(body, axes),
        mesh=mesh,
        in_specs=placed,
        out_specs=(P(None, "shard", None), P(None, "shard", "replica")),
        check_vma=False,
    )
```

time: 236 us -> 86.2 us (0.37)
  blocking collectives: 123 us -> 0 us
  Pallas kernels: 0 us -> 80.4 us
  waiting for transfers between devices: 61.3 us -> 0 us
  matrix products: 33.9 us -> 0 us
  between operations: 14.2 us -> 0.65 us
  local copies, waits for them, and re-layouts: 1.94 us -> 4.34 us
    all_to_all x2 -> x0, blocking collectives: 123 us -> none  [the longest x1 88.4 us: summed_on_arrival(): lax.all_to_all(parts, axis, split_axis=0, concat_axis=0, tiled=True)]
    pallas_call x0 -> x1, Pallas kernels: none -> 80.4 us  [body(): pl.pallas_call(functools.partial(kernel, n, axes), out_shape=(jax.ShapeDt...]
    all_gather x1 -> x0, waiting for transfers between devices: 61.3 us -> none  [body(): lax.all_gather(direction.astype(jnp.bfloat16), 'replica', axis=2, tiled=T...]
    dot_general x15 -> x0, matrix products: 33.9 us -> none  [the longest x5 16.8 us: polish(): jnp.einsum('lbij,lbjk->lbik', mixture, blocks, precision=EXACTNESS)]
    unnamed x5 -> x6, local copies, waits for them, and re-layouts: 1.72 us -> 4.34 us
  transfers between devices with their start and end apart: 1 -> 0, of which waited for: 1 -> 0; matrix products, arithmetic and copies ran while one was open for 0% -> 0% of each run, Pallas kernels for 0% -> 0%
where the time goes in v2:
time: 86.2 us; the launch traced here: 85.4 us
  Pallas kernels  80.4 us (93%)
  local copies, waits for them, and re-layouts  4.34 us (5%)
    pallas_call x1, Pallas kernels, body(): pl.pallas_call(functools.partial(kernel, n, axes), out_shape=(jax.ShapeDt...  80.4 us
    unnamed x6, local copies, waits for them, and re-layouts  4.34 us

profile of v2, /device:TPU:1, one launch (start us, length us, event | category | flops | bytes accessed | tf_op | source)
XLA Modules:
  0.0 85.4 jit_solution(5490149365122747812)
XLA Ops:
  0.6 0.0 copy-start
  0.6 1.4 %copy-done = bf16[1,2,80,5120]{3,2,1,0:T(8,128)(2,1)S(1)} copy-done((bf16[1,2,80,5120]{3,2,1,0:T(8,128)(2,1)S(1)}, bf16[1,2,80,5120]{3,2,1,0:T(8,128)(2,1)}, u32[]{:S(2)}) %copy-start) | copy-done | bytes 1638424
  2.1 0.0 copy-start.1
  2.1 1.0 %copy-done.1 = f32[2,80,640]{2,1,0:T(8,128)S(1)} copy-done((f32[2,80,640]{2,1,0:T(8,128)S(1)}, f32[2,80,640]{2,1,0:T(8,128)}, u32[]{:S(2)}) %copy-start.1) | copy-done | bytes 409624
  3.1 80.4 %shard_map.41 = (bf16[2,80,5120]{2,1,0:T(8,128)(2,1)S(1)}, f32[2,80,640]{2,1,0:T(8,128)S(1)}) custom-call(bf16[1,2,80,5120]{3,2,1,0:T(8,128)(2,1)S(1)} %copy-done, f32[2,80,640]{2,1,0:T(8,128)S(1)} %copy-done.1), custom_call_target="tpu_custom_call" | custom-call | tf_op jit(solution)/shard_map/pallas_call | solution.py:306
  83.5 1.2 %copy.6 = bf16[2,80,5120]{2,1,0:T(8,128)(2,1)} copy(bf16[2,80,5120]{2,1,0:T(8,128)(2,1)S(1)} %get-tuple-element.4) | data formatting | bytes 3276800
  84.6 0.8 copy.7
Async XLA Ops:
  0.6 1.4 %copy-start = (bf16[1,2,80,5120]{3,2,1,0:T(8,128)(2,1)S(1)}, bf16[1,2,80,5120]{3,2,1,0:T(8,128)(2,1)}, u32[]{:S(2)}) copy-start(bf16[1,2,80,5120]{3,2,1,0:T(8,128)(2,1)} %grads_hbm.1) | copy-start | bytes 4915204
  2.1 1.0 %copy-start.1 = (f32[2,80,640]{2,1,0:T(8,128)S(1)}, f32[2,80,640]{2,1,0:T(8,128)}, u32[]{:S(2)}) copy-start(f32[2,80,640]{2,1,0:T(8,128)} %moment_hbm.1) | copy-start | bytes 1228804

commit v3 on v2

v3 whole, which is shorter than its diff:
```python
import functools
import math

import jax
import jax.numpy as jnp
from jax import lax
from jax.experimental import pallas as pl
from jax.experimental.pallas import tpu as pltpu
from jax.sharding import PartitionSpec as P

ITERS = 5
QUINTIC_FIRST = 3.4445
QUINTIC_SECOND = -4.775
QUINTIC_THIRD = 2.0315
MOMENTUM_RATE = 0.9
EPSILON = 1e-07
EXACTNESS = lax.Precision.HIGHEST
MESH = pl.DeviceIdType.MESH

SHARD_AXES = (2, 4, 4, 2)
TILE = 128
EARLY = 8
PIECES = 4
GROUP = 8
LAG = 9


def rates(n):
    gain = (1.0 + MOMENTUM_RATE) / n
    return gain, MOMENTUM_RATE * MOMENTUM_RATE / gain


def kernel(
    n, axes, grads_hbm, moment_hbm, gathered, mix_out,
    grads, moment, inward_part, cross_part, gram, squares, plane_in, ring_in,
    load_sem, inward_recv, cross_recv, outward_recv, inward_send, outward_send,
    plane_send, plane_recv, ring_send, ring_recv,
):
    halves, xs, ys, cores = axes
    layers, rows, cols = grads.shape
    width = cols // n
    per_layer = cols // TILE
    messages = layers * per_layer
    ring = halves * n
    middle = n // 2 - 1

    gain, mixed = rates(n)

    i = lax.axis_index("replica")
    shard = lax.axis_index("shard")
    half = lax.div(shard, cores * ys * xs)
    z = half * n + i
    in_plane = shard - half * (cores * ys * xs)
    upper = lax.div(i, n // 2)
    depth = i + upper * (n - 1 - 2 * i)
    inward = (i + 1 - 2 * upper, shard)
    outward = (i - 1 + 2 * upper, shard)

    def along_z(offset):
        there = lax.rem(z + offset, ring)
        return (lax.rem(there, n), lax.div(there, n) * (cores * ys * xs) + in_plane)

    plane = xs * ys * cores
    offsets = range(1, plane)

    def across(offset):
        return (i, half * plane + lax.rem(in_plane + offset, plane))

    loads = [
        pltpu.make_async_copy(moment_hbm, moment, load_sem.at[0]),
        pltpu.make_async_copy(grads_hbm.at[0], grads, load_sem.at[1]),
    ]
    for load in loads:
        load.start()

    barrier = pltpu.get_barrier_semaphore()
    pl.semaphore_signal(barrier, inc=1, device_id=inward, device_id_type=MESH)

    @pl.when(depth > 0)
    def _():
        pl.semaphore_signal(barrier, inc=1, device_id=outward, device_id_type=MESH)

    if halves > 1:
        far = (n // 2 - upper, lax.rem(half + 1, halves) * (cores * ys * xs) + in_plane)
        pl.semaphore_signal(barrier, inc=1, device_id=far, device_id_type=MESH)

    @pl.when(depth == middle)
    def _():
        for offset in offsets:
            pl.semaphore_signal(barrier, inc=1, device_id=across(offset), device_id_type=MESH)

    def place(ref, m):
        column = pl.multiple_of(lax.rem(lax.rem(m, per_layer) + EARLY, per_layer) * TILE, TILE)
        return ref.at[lax.div(m, per_layer), :, pl.ds(column, TILE)]

    def inward_copy(m, source):
        return pltpu.make_async_remote_copy(
            src_ref=source, dst_ref=inward_part.at[m], send_sem=inward_send, recv_sem=inward_recv.at[m],
            device_id=inward, device_id_type=MESH)

    def cross_copy(m):
        return pltpu.make_async_remote_copy(
            src_ref=inward_part.at[m], dst_ref=cross_part.at[m], send_sem=inward_send,
            recv_sem=cross_recv.at[m], device_id=inward, device_id_type=MESH)

    def outward_copy(m):
        chunk = place(gathered, m)
        return pltpu.make_async_remote_copy(
            src_ref=chunk, dst_ref=chunk, send_sem=outward_send, recv_sem=outward_recv.at[m],
            device_id=outward, device_id_type=MESH)

    def send_inward(m):
        own = place(grads, m)

        @pl.when((depth == 0) & (m >= EARLY))
        def _():
            inward_copy(m, own).start()

        @pl.when(depth > 0)
        def _():
            inward_copy(m, own).wait_recv()
            total = inward_part[m].astype(jnp.float32) + own[...].astype(jnp.float32)
            inward_part[m] = total.astype(jnp.bfloat16)

            @pl.when(depth < middle)
            def _():
                inward_copy(m, inward_part.at[m]).start()

            @pl.when(depth == middle)
            def _():
                cross_copy(m).start()

    def send_outward(m):
        @pl.when(depth == middle)
        def _():
            cross_copy(m).wait_recv()
            total = inward_part[m].astype(jnp.float32) + cross_part[m].astype(jnp.float32)
            place(gathered, m)[...] = total.astype(jnp.bfloat16)
            outward_copy(m).start()
            squares[0, pl.ds(lax.div(m, per_layer), 1), :] += jnp.sum(total * total, axis=0, keepdims=True)

        @pl.when(depth < middle)
        def _():
            outward_copy(m).wait_recv()

            @pl.when(depth > 0)
            def _():
                outward_copy(m).start()

        @pl.when(lax.rem(m, GROUP) == GROUP - 1)
        def _():
            k = lax.div(m, per_layer)
            first = lax.rem(lax.rem(m, per_layer) - (GROUP - 1) + EARLY, per_layer)
            first = pl.multiple_of(first * TILE, TILE)
            band = gathered[k, :, pl.ds(first, GROUP * TILE)]
            gram[k] += lax.dot_general(band, band, (((1,), (1,)), ((), ())), preferred_element_type=jnp.float32)

    gram[...] = jnp.zeros_like(gram)
    squares[...] = jnp.zeros_like(squares)

    @pl.when(depth == 0)
    def _():
        pl.semaphore_wait(barrier, 1)
        for m in range(EARLY):
            inward_copy(m, place(grads_hbm.at[0], m)).start()

    for load in loads:
        load.wait()
    mine = pl.ds(pl.multiple_of(i * width, TILE), width)
    for k in range(layers):
        own = grads[k, :, mine].astype(jnp.float32) + mixed * moment[k]
        grads[k, :, mine] = own.astype(jnp.bfloat16)

    @pl.when((depth > 0) & (depth < middle))
    def _():
        pl.semaphore_wait(barrier, 2)

    @pl.when(depth == middle)
    def _():
        pl.semaphore_wait(barrier, 2 + len(offsets) + (halves - 1) * (n // 2))

    wait_for = (2 * middle + 1 - 2 * depth) * LAG

    def step(t, carry):
        @pl.when(t < messages)
        def _():
            send_inward(t)

        @pl.when(t >= wait_for)
        def _():
            send_outward(t - wait_for)

        return carry

    lax.fori_loop(0, messages + wait_for, step, 0)

    def plane_copies():
        return [
            pltpu.make_async_remote_copy(
                src_ref=squares.at[0], dst_ref=plane_in.at[at], send_sem=plane_send.at[at],
                recv_sem=plane_recv.at[at], device_id=across(offset), device_id_type=MESH)
            for at, offset in enumerate(offsets)
        ]

    reach = ring // 2

    def ring_copy(offset):
        return pltpu.make_async_remote_copy(
            src_ref=squares.at[1], dst_ref=ring_in.at[half], send_sem=ring_send.at[offset],
            recv_sem=ring_recv.at[half], device_id=along_z(lax.rem(ring + (2 * upper - 1) * offset, ring)),
            device_id_type=MESH)

    def ring_arrival(source):
        return pltpu.make_async_remote_copy(
            src_ref=squares.at[1], dst_ref=ring_in.at[source], send_sem=ring_send.at[0],
            recv_sem=ring_recv.at[source], device_id=inward, device_id_type=MESH)

    @pl.when(depth == middle)
    def _():
        copies = plane_copies()
        for copy in copies:
            copy.start()
        total = squares[0]
        for at, copy in enumerate(copies):
            copy.wait_recv()
            total = total + plane_in[at]
        squares[1] = total
        for offset in range(1, reach):
            ring_copy(offset).start()

    pltpu.make_async_copy(grads, grads, inward_send).wait()

    @pl.when(depth > 0)
    def _():
        pltpu.make_async_copy(grads, grads, outward_send).wait()

    for source in range(halves):
        @pl.when((depth == middle) & (half == source))
        def _():
            ring_in[source] = squares[1]

        @pl.when((depth != middle) | (half != source))
        def _():
            ring_arrival(source).wait_recv()

    total = ring_in[0]
    for source in range(1, halves):
        total = total + ring_in[source]

    eye = (lax.broadcasted_iota(jnp.int32, (rows, rows), 0) == lax.broadcasted_iota(jnp.int32, (rows, rows), 1))
    eye = eye.astype(jnp.float32)
    product = functools.partial(jnp.dot, precision=EXACTNESS, preferred_element_type=jnp.float32)
    factors, states, mixes = [], [], []
    for k in range(layers):
        norm = gain * jnp.sqrt(jnp.sum(total[k : k + 1, :], axis=1, keepdims=True))
        factor = gain / (norm + EPSILON)
        factors.append(factor)
        states.append(gram[k] * (factor * factor))
        mixes.append(None)
    for iteration in range(ITERS):
        for k in range(layers):
            state = states[k]
            square = product(state, state)
            poly = QUINTIC_FIRST * eye + QUINTIC_SECOND * state + QUINTIC_THIRD * square
            mixes[k] = poly if mixes[k] is None else product(poly, mixes[k])
            if iteration + 1 < ITERS:
                states[k] = product(product(state, poly), poly)

    for k in range(layers):
        mix_out[k] = mixes[k] * (factors[k] * math.sqrt(cols))

    @pl.when(depth == middle)
    def _():
        for copy in plane_copies():
            copy.wait_send()
        for offset in range(1, reach):
            ring_copy(offset).wait_send()


def finish(n, gathered, mix, moment_hbm, out_hbm, next_hbm, moment, fresh, result, load_sem, store_sem):
    layers, rows, cols = gathered.shape
    width = cols // n
    mixed = rates(n)[1]
    load = pltpu.make_async_copy(moment_hbm, moment, load_sem)
    load.start()
    span = cols // PIECES
    stores = []
    for k in range(layers):
        high = mix[k].astype(jnp.bfloat16)
        low = (mix[k] - high.astype(jnp.float32)).astype(jnp.bfloat16)
        both = jnp.concatenate([high, low], axis=0)
        for at in range(PIECES):
            window = pl.ds(at * span, span)
            value = jnp.dot(both, gathered[k, :, window], preferred_element_type=jnp.float32)
            result[k, :, window] = (value[:rows] + value[rows:]).astype(jnp.bfloat16)
            stores.append(pltpu.make_async_copy(
                result.at[k, :, window], out_hbm.at[k, :, window], store_sem.at[1 + k * PIECES + at]))
            stores[-1].start()
        if k == 0:
            load.wait()
            mine = pl.ds(pl.multiple_of(lax.axis_index("replica") * width, TILE), width)
            for every in range(layers):
                average = (gathered[every, :, mine].astype(jnp.float32) - mixed * moment[every]) / n
                fresh[every] = MOMENTUM_RATE * moment[every] + average
            stores.append(pltpu.make_async_copy(fresh, next_hbm, store_sem.at[0]))
            stores[-1].start()
    for store in stores:
        store.wait()


def body(axes, pseudo_grads, momentum):
    n = lax.axis_size("replica")
    _, layers, rows, cols = pseudo_grads.shape
    width = cols // n
    messages = layers * cols // TILE
    ring = axes[0] * n
    plane = max(axes[1] * axes[2] * axes[3] - 1, 1)
    dma = pltpu.SemaphoreType.DMA
    any_spec = pl.BlockSpec(memory_space=pl.ANY)
    vmem_spec = pl.BlockSpec(memory_space=pltpu.VMEM)
    bf16, f32 = jnp.bfloat16, jnp.float32
    momentum = pltpu.with_memory_space_constraint(momentum, pltpu.HBM)
    gathered, mix = pl.pallas_call(
        functools.partial(kernel, n, axes),
        out_shape=(
            jax.ShapeDtypeStruct((layers, rows, cols), bf16),
            jax.ShapeDtypeStruct((layers, rows, rows), f32),
        ),
        in_specs=[any_spec, any_spec],
        out_specs=(vmem_spec, vmem_spec),
        scratch_shapes=[
            pltpu.VMEM((layers, rows, cols), bf16),
            pltpu.VMEM((layers, rows, width), f32),
            pltpu.VMEM((messages, rows, TILE), bf16),
            pltpu.VMEM((messages, rows, TILE), bf16),
            pltpu.VMEM((layers, rows, rows), f32),
            pltpu.VMEM((2, 2, TILE), f32),
            pltpu.VMEM((plane, 2, TILE), f32),
            pltpu.VMEM((axes[0], 2, TILE), f32),
            dma((2,)),
            dma((messages,)),
            dma((messages,)),
            dma((messages,)),
            dma,
            dma,
            dma((plane,)),
            dma((plane,)),
            dma((ring,)),
            dma((axes[0],)),
        ],
        compiler_params=pltpu.CompilerParams(
            collective_id=0, has_side_effects=True, vmem_limit_bytes=40 * 1024 * 1024),
    )(pltpu.with_memory_space_constraint(pseudo_grads, pltpu.HBM), momentum)
    return pl.pallas_call(
        functools.partial(finish, n),
        out_shape=(
            jax.ShapeDtypeStruct((layers, rows, cols), bf16),
            jax.ShapeDtypeStruct((layers, rows, width), f32),
        ),
        in_specs=[vmem_spec, vmem_spec, any_spec],
        out_specs=(any_spec, any_spec),
        scratch_shapes=[
            pltpu.VMEM((layers, rows, width), f32),
            pltpu.VMEM((layers, rows, width), f32),
            pltpu.VMEM((layers, rows, cols), bf16),
            dma,
            dma((1 + layers * PIECES,)),
        ],
        compiler_params=pltpu.CompilerParams(vmem_limit_bytes=40 * 1024 * 1024),
    )(gathered, mix, momentum)


def solution(mesh, axes=SHARD_AXES):
    placed = (P("replica", None, "shard", None), P(None, "shard", "replica"))
    return jax.shard_map(
        functools.partial(body, axes),
        mesh=mesh,
        in_specs=placed,
        out_specs=(P(None, "shard", None), P(None, "shard", "replica")),
        check_vma=False,
    )
```

time: 86.2 us -> 77.6 us (0.900)
  local copies, waits for them, and re-layouts: 4.34 us -> 0 us
  Pallas kernels: 80.4 us -> 76.7 us
    pallas_call x1, Pallas kernels: 80.4 us -> 74.3 us  [body(): pl.pallas_call(functools.partial(kernel, n, axes), out_shape=(jax.ShapeDt...]
    unnamed x6 -> x0, local copies, waits for them, and re-layouts: 4.34 us -> none
    pallas_call x0 -> x1, Pallas kernels: none -> 2.44 us  [body(): pl.pallas_call(functools.partial(finish, n), out_shape=(jax.ShapeDtypeStr...]
where the time goes in v3:
time: 77.6 us; the launch traced here: 77.4 us
  Pallas kernels  76.7 us (99%)
    pallas_call x1, Pallas kernels, body(): pl.pallas_call(functools.partial(kernel, n, axes), out_shape=(jax.ShapeDt...  74.3 us
    pallas_call x1, Pallas kernels, body(): pl.pallas_call(functools.partial(finish, n), out_shape=(jax.ShapeDtypeStr...  2.44 us

profile of v3, /device:TPU:1, one launch (start us, length us, event | category | flops | bytes accessed | tf_op | source)
XLA Modules:
  0.0 77.4 jit_solution(2601883399252947434)
XLA Ops:
  0.6 74.3 %shard_map.41 = (bf16[2,80,5120]{2,1,0:T(8,128)(2,1)S(1)}, f32[2,80,80]{2,1,0:T(8,128)S(1)}) custom-call(bf16[1,2,80,5120]{3,2,1,0:T(8,128)(2,1)} %grads_hbm.1, f32[2,80,640]{2,1,0:T(8,128)} %moment_hbm.3), custom_call_target="tpu_custom_call" | custom-call | tf_op jit(solution)/shard_map/pallas_call | solution.py:323
  74.9 2.4 %shard_map.42 = (bf16[2,80,5120]{2,1,0:T(8,128)(2,1)}, f32[2,80,640]{2,1,0:T(8,128)}) custom-call(bf16[2,80,5120]{2,1,0:T(8,128)(2,1)S(1)} %get-tuple-element.4.gathered, f32[2,80,80]{2,1,0:T(8,128)S(1)} %get-tuple-element.5.mix, f32[2,80,640]{2,1,0:T(8,128)} %moment_hbm.3), custom_call_target="tpu_custom_call" | custom-call | tf_op jit(solution)/shard_map/pallas_call | solution.py:354

commit v4 on v3

--- a/solution.py
+++ b/solution.py
@@ -14,15 +14,20 @@
 QUINTIC_THIRD = 2.0315
 MOMENTUM_RATE = 0.9
 EPSILON = 1e-07
+TINY = 1e-30
 EXACTNESS = lax.Precision.HIGHEST
 MESH = pl.DeviceIdType.MESH
 
 SHARD_AXES = (2, 4, 4, 2)
-TILE = 128
-EARLY = 8
+LANES = 128
+TILE = 256
+EARLY = 4
 PIECES = 4
-GROUP = 8
-LAG = 9
+GROUP = 4
+LAG_MIDDLE = 5
+BURST = 4
+SETTLE = 14
+LAG = 5
 
 
 def rates(n):
@@ -31,7 +36,7 @@
 
 
 def kernel(
-    n, axes, grads_hbm, moment_hbm, gathered, mix_out,
+    n, axes, grads_hbm, moment_hbm, gathered, mix_out, done_out,
     grads, moment, inward_part, cross_part, gram, squares, plane_in, ring_in,
     load_sem, inward_recv, cross_recv, outward_recv, inward_send, outward_send,
     plane_send, plane_recv, ring_send, ring_recv,
@@ -137,7 +142,7 @@
             total = inward_part[m].astype(jnp.float32) + cross_part[m].astype(jnp.float32)
             place(gathered, m)[...] = total.astype(jnp.bfloat16)
             outward_copy(m).start()
-            squares[0, pl.ds(lax.div(m, per_layer), 1), :] += jnp.sum(total * total, axis=0, keepdims=True)
+            squares[0, lax.div(m, per_layer)] += jnp.sum(total * total, axis=0, keepdims=True)
 
         @pl.when(depth < middle)
         def _():
@@ -166,7 +171,7 @@
 
     for load in loads:
         load.wait()
-    mine = pl.ds(pl.multiple_of(i * width, TILE), width)
+    mine = pl.ds(pl.multiple_of(i * width, LANES), width)
     for k in range(layers):
         own = grads[k, :, mine].astype(jnp.float32) + mixed * moment[k]
         grads[k, :, mine] = own.astype(jnp.bfloat16)
@@ -179,7 +184,47 @@
     def _():
         pl.semaphore_wait(barrier, 2 + len(offsets) + (halves - 1) * (n // 2))
 
-    wait_for = (2 * middle + 1 - 2 * depth) * LAG
+    wait_for = (2 * middle + 1 - 2 * depth) * LAG - lax.div(depth, middle) * (LAG - LAG_MIDDLE)
+
+    def plane_copy(k, offset):
+        return pltpu.make_async_remote_copy(
+            src_ref=squares.at[0, k], dst_ref=plane_in.at[k, offset - 1], send_sem=plane_send.at[k],
+            recv_sem=plane_recv.at[k], device_id=across(offset), device_id_type=MESH)
+
+    reach = ring // 2
+
+    def ring_copy(k, offset):
+        return pltpu.make_async_remote_copy(
+            src_ref=squares.at[1, k], dst_ref=ring_in.at[k, half], send_sem=ring_send.at[k, offset],
+            recv_sem=ring_recv.at[k, half], device_id=along_z(lax.rem(ring + (2 * upper - 1) * offset, ring)),
+            device_id_type=MESH)
+
+    def plane_sum(k):
+        if plane > 1:
+            pltpu.make_async_copy(plane_in.at[k], plane_in.at[k], plane_recv.at[k]).wait()
+        total = squares[0, k]
+        for at in range(plane - 1):
+            total = total + plane_in[k, at]
+        squares[1, k] = total
+        for offset in range(1, reach):
+            ring_copy(k, offset).start()
+
+    def norm_factor(k):
+        total = jnp.zeros((1, TILE), jnp.float32)
+        for source in range(halves):
+            @pl.when((depth == middle) & (half == source))
+            def _():
+                ring_in[k, source] = squares[1, k]
+
+            @pl.when((depth != middle) | (half != source))
+            def _():
+                pltpu.make_async_remote_copy(
+                    src_ref=squares.at[1, k], dst_ref=ring_in.at[k, source], send_sem=ring_send.at[k, 0],
+                    recv_sem=ring_recv.at[k, source], device_id=inward, device_id_type=MESH).wait_recv()
+
+            total = total + ring_in[k, source]
+        norm = gain * jnp.sqrt(jnp.sum(total, axis=1, keepdims=True))
+        return gain / (norm + EPSILON)
 
     def step(t, carry):
         @pl.when(t < messages)
@@ -190,120 +235,126 @@
         def _():
             send_outward(t - wait_for)
 
+        for k in range(layers - 1):
+            since = t - wait_for - (k + 1) * per_layer
+
+            for q in range(BURST):
+                @pl.when((depth == middle) & (since >= 0) & (since * BURST + q + 1 < plane))
+                def _():
+                    plane_copy(k, since * BURST + q + 1).start()
+
+            @pl.when((depth == middle) & (since == SETTLE))
+            def _():
+                plane_sum(k)
+
         return carry
 
     lax.fori_loop(0, messages + wait_for, step, 0)
-
-    def plane_copies():
-        return [
-            pltpu.make_async_remote_copy(
-                src_ref=squares.at[0], dst_ref=plane_in.at[at], send_sem=plane_send.at[at],
-                recv_sem=plane_recv.at[at], device_id=across(offset), device_id_type=MESH)
-            for at, offset in enumerate(offsets)
-        ]
-
-    reach = ring // 2
-
-    def ring_copy(offset):
-        return pltpu.make_async_remote_copy(
-            src_ref=squares.at[1], dst_ref=ring_in.at[half], send_sem=ring_send.at[offset],
-            recv_sem=ring_recv.at[half], device_id=along_z(lax.rem(ring + (2 * upper - 1) * offset, ring)),
-            device_id_type=MESH)
-
-    def ring_arrival(source):
-        return pltpu.make_async_remote_copy(
-            src_ref=squares.at[1], dst_ref=ring_in.at[source], send_sem=ring_send.at[0],
-            recv_sem=ring_recv.at[source], device_id=inward, device_id_type=MESH)
-
-    @pl.when(depth == middle)
-    def _():
-        copies = plane_copies()
-        for copy in copies:
-            copy.start()
-        total = squares[0]
-        for at, copy in enumerate(copies):
-            copy.wait_recv()
-            total = total + plane_in[at]
-        squares[1] = total
-        for offset in range(1, reach):
-            ring_copy(offset).start()
-
-    pltpu.make_async_copy(grads, grads, inward_send).wait()
-
-    @pl.when(depth > 0)
-    def _():
-        pltpu.make_async_copy(grads, grads, outward_send).wait()
-
-    for source in range(halves):
-        @pl.when((depth == middle) & (half == source))
-        def _():
-            ring_in[source] = squares[1]
-
-        @pl.when((depth != middle) | (half != source))
-        def _():
-            ring_arrival(source).wait_recv()
-
-    total = ring_in[0]
-    for source in range(1, halves):
-        total = total + ring_in[source]
 
     eye = (lax.broadcasted_iota(jnp.int32, (rows, rows), 0) == lax.broadcasted_iota(jnp.int32, (rows, rows), 1))
     eye = eye.astype(jnp.float32)
     product = functools.partial(jnp.dot, precision=EXACTNESS, preferred_element_type=jnp.float32)
-    factors, states, mixes = [], [], []
-    for k in range(layers):
-        norm = gain * jnp.sqrt(jnp.sum(total[k : k + 1, :], axis=1, keepdims=True))
-        factor = gain / (norm + EPSILON)
-        factors.append(factor)
-        states.append(gram[k] * (factor * factor))
-        mixes.append(None)
-    for iteration in range(ITERS):
+
+    def polynomial(state, square):
+        return QUINTIC_FIRST * eye + QUINTIC_SECOND * state + QUINTIC_THIRD * square
+
+    def newton_schulz(state, mix, count):
+        for iteration in range(count):
+            poly = polynomial(state, product(state, state))
+            mix = poly if mix is None else product(poly, mix)
+            if iteration + 1 < count:
+                state = product(product(state, poly), poly)
+        return mix
+
+    final = layers - 1
+
+    @pl.when(depth == middle)
+    def _():
+        for offset in offsets:
+            plane_copy(final, offset).start()
+
+    early = []
+    for k in range(final):
+        factor = norm_factor(k)
+        early.append(newton_schulz(gram[k] * (factor * factor), None, ITERS) * (factor * math.sqrt(cols)))
+
+    @pl.when(depth == middle)
+    def _():
+        plane_sum(final)
+
+    for k in range(final):
+        apply_mix(early[k], gathered, k, lambda window, value: done_out.__setitem__((k, slice(None), window), value))
+
+    trace = jnp.sum(gram[final] * eye, axis=(0, 1), keepdims=True) + TINY
+    one = gram[final] / trace
+    two = product(one, one)
+    three, four = product(one, two), product(two, two)
+    five = product(two, three)
+    a, b, c = QUINTIC_FIRST, QUINTIC_SECOND, QUINTIC_THIRD
+    factor = norm_factor(final)
+    share = factor * factor * trace
+    mix = polynomial(share * one, (share * share) * two)
+    state = share * (
+        a * a * one
+        + share * (2.0 * a * b * two
+        + share * ((b * b + 2.0 * a * c) * three
+        + share * (2.0 * b * c * four
+        + share * (c * c * five)))))
+    mix = newton_schulz(state, mix, ITERS - 1)
+    mix_out[...] = mix * (factor * math.sqrt(cols))
+
+    pltpu.make_async_copy(grads, grads, inward_send).wait()
+
+    @pl.when(depth > 0)
+    def _():
+        pltpu.make_async_copy(grads, grads, outward_send).wait()
+
+    @pl.when(depth == middle)
+    def _():
         for k in range(layers):
-            state = states[k]
-            square = product(state, state)
-            poly = QUINTIC_FIRST * eye + QUINTIC_SECOND * state + QUINTIC_THIRD * square
-            mixes[k] = poly if mixes[k] is None else product(poly, mixes[k])
-            if iteration + 1 < ITERS:
-                states[k] = product(product(state, poly), poly)
-
-    for k in range(layers):
-        mix_out[k] = mixes[k] * (factors[k] * math.sqrt(cols))
-
-    @pl.when(depth == middle)
-    def _():
-        for copy in plane_copies():
-            copy.wait_send()
-        for offset in range(1, reach):
-            ring_copy(offset).wait_send()
-
-
-def finish(n, gathered, mix, moment_hbm, out_hbm, next_hbm, moment, fresh, result, load_sem, store_sem):
+            if plane > 1:
+                pltpu.make_async_copy(plane_in.at[k], plane_in.at[k], plane_send.at[k]).wait()
+            for offset in range(1, reach):
+                ring_copy(k, offset).wait_send()
+
+
+def apply_mix(mix, gathered, k, put):
+    rows, cols = gathered.shape[1:]
+    high = mix.astype(jnp.bfloat16)
+    low = (mix - high.astype(jnp.float32)).astype(jnp.bfloat16)
+    both = jnp.concatenate([high, low], axis=0)
+    span = cols // PIECES
+    for at in range(PIECES):
+        window = pl.ds(at * span, span)
+        value = jnp.dot(both, gathered[k, :, window], preferred_element_type=jnp.float32)
+        put(window, (value[:rows] + value[rows:]).astype(jnp.bfloat16))
+
+
+def finish(n, gathered, mix, done, moment_hbm, out_hbm, next_hbm, moment, fresh, result, load_sem, store_sem):
     layers, rows, cols = gathered.shape
     width = cols // n
+    final = layers - 1
     mixed = rates(n)[1]
     load = pltpu.make_async_copy(moment_hbm, moment, load_sem)
     load.start()
-    span = cols // PIECES
-    stores = []
+    stores = [pltpu.make_async_copy(done, out_hbm.at[pl.ds(0, final)], store_sem.at[0])]
+    stores[-1].start()
+
+    def put(window, value):
+        result[:, window] = value
+        store = pltpu.make_async_copy(
+            result.at[:, window], out_hbm.at[final, :, window], store_sem.at[len(stores)])
+        store.start()
+        stores.append(store)
+
+    apply_mix(mix[...], gathered, final, put)
+    load.wait()
+    mine = pl.ds(pl.multiple_of(lax.axis_index("replica") * width, LANES), width)
     for k in range(layers):
-        high = mix[k].astype(jnp.bfloat16)
-        low = (mix[k] - high.astype(jnp.float32)).astype(jnp.bfloat16)
-        both = jnp.concatenate([high, low], axis=0)
-        for at in range(PIECES):
-            window = pl.ds(at * span, span)
-            value = jnp.dot(both, gathered[k, :, window], preferred_element_type=jnp.float32)
-            result[k, :, window] = (value[:rows] + value[rows:]).astype(jnp.bfloat16)
-            stores.append(pltpu.make_async_copy(
-                result.at[k, :, window], out_hbm.at[k, :, window], store_sem.at[1 + k * PIECES + at]))
-            stores[-1].start()
-        if k == 0:
-            load.wait()
-            mine = pl.ds(pl.multiple_of(lax.axis_index("replica") * width, TILE), width)
-            for every in range(layers):
-                average = (gathered[every, :, mine].astype(jnp.float32) - mixed * moment[every]) / n
-                fresh[every] = MOMENTUM_RATE * moment[every] + average
-            stores.append(pltpu.make_async_copy(fresh, next_hbm, store_sem.at[0]))
-            stores[-1].start()
+        average = (gathered[k, :, mine].astype(jnp.float32) - mixed * moment[k]) / n
+        fresh[k] = MOMENTUM_RATE * moment[k] + average
+        stores.append(pltpu.make_async_copy(fresh.at[k], next_hbm.at[k], store_sem.at[len(stores)]))
+        stores[-1].start()
     for store in stores:
         store.wait()
 
@@ -320,33 +371,34 @@
     vmem_spec = pl.BlockSpec(memory_space=pltpu.VMEM)
     bf16, f32 = jnp.bfloat16, jnp.float32
     momentum = pltpu.with_memory_space_constraint(momentum, pltpu.HBM)
-    gathered, mix = pl.pallas_call(
+    gathered, mix, done = pl.pallas_call(
         functools.partial(kernel, n, axes),
         out_shape=(
             jax.ShapeDtypeStruct((layers, rows, cols), bf16),
-            jax.ShapeDtypeStruct((layers, rows, rows), f32),
+            jax.ShapeDtypeStruct((rows, rows), f32),
+            jax.ShapeDtypeStruct((layers - 1, rows, cols), bf16),
         ),
         in_specs=[any_spec, any_spec],
-        out_specs=(vmem_spec, vmem_spec),
+        out_specs=(vmem_spec, vmem_spec, vmem_spec),
         scratch_shapes=[
             pltpu.VMEM((layers, rows, cols), bf16),
             pltpu.VMEM((layers, rows, width), f32),
             pltpu.VMEM((messages, rows, TILE), bf16),
             pltpu.VMEM((messages, rows, TILE), bf16),
             pltpu.VMEM((layers, rows, rows), f32),
-            pltpu.VMEM((2, 2, TILE), f32),
-            pltpu.VMEM((plane, 2, TILE), f32),
-            pltpu.VMEM((axes[0], 2, TILE), f32),
+            pltpu.VMEM((2, layers, 1, TILE), f32),
+            pltpu.VMEM((layers, plane, 1, TILE), f32),
+            pltpu.VMEM((layers, axes[0], 1, TILE), f32),
             dma((2,)),
             dma((messages,)),
             dma((messages,)),
             dma((messages,)),
             dma,
             dma,
-            dma((plane,)),
-            dma((plane,)),
-            dma((ring,)),
-            dma((axes[0],)),
+            dma((layers,)),
+            dma((layers,)),
+            dma((layers, ring)),
+            dma((layers, axes[0])),
         ],
         compiler_params=pltpu.CompilerParams(
             collective_id=0, has_side_effects=True, vmem_limit_bytes=40 * 1024 * 1024),
@@ -357,17 +409,17 @@
             jax.ShapeDtypeStruct((layers, rows, cols), bf16),
             jax.ShapeDtypeStruct((layers, rows, width), f32),
         ),
-        in_specs=[vmem_spec, vmem_spec, any_spec],
+        in_specs=[vmem_spec, vmem_spec, vmem_spec, any_spec],
         out_specs=(any_spec, any_spec),
         scratch_shapes=[
             pltpu.VMEM((layers, rows, width), f32),
             pltpu.VMEM((layers, rows, width), f32),
-            pltpu.VMEM((layers, rows, cols), bf16),
+            pltpu.VMEM((rows, cols), bf16),
             dma,
-            dma((1 + layers * PIECES,)),
+            dma((1 + layers + PIECES,)),
         ],
         compiler_params=pltpu.CompilerParams(vmem_limit_bytes=40 * 1024 * 1024),
-    )(gathered, mix, momentum)
+    )(gathered, mix, done, momentum)
 
 
 def solution(mesh, axes=SHARD_AXES):

time: 77.6 us -> 75.7 us (0.976)
  Pallas kernels: 76.7 us -> 74.9 us
    pallas_call x1, Pallas kernels: 74.3 us -> 72.7 us  [body(): pl.pallas_call(functools.partial(kernel, n, axes), out_shape=(jax.ShapeDt...]
where the time goes in v4:
time: 75.7 us; the launch traced here: 75.5 us
  Pallas kernels  74.9 us (99%)
    pallas_call x1, Pallas kernels, body(): pl.pallas_call(functools.partial(kernel, n, axes), out_shape=(jax.ShapeDt...  72.7 us
    pallas_call x1, Pallas kernels, body(): pl.pallas_call(functools.partial(finish, n), out_shape=(jax.ShapeDtypeStr...  2.13 us

profile of v4, /device:TPU:1, one launch (start us, length us, event | category | flops | bytes accessed | tf_op | source)
XLA Modules:
  0.0 75.5 jit_solution(11466414460960950884)
XLA Ops:
  0.6 72.7 %shard_map.41 = (bf16[2,80,5120]{2,1,0:T(8,128)(2,1)S(1)}, f32[80,80]{1,0:T(8,128)S(1)}, bf16[1,80,5120]{2,1,0:T(8,128)(2,1)S(1)}) custom-call(bf16[1,2,80,5120]{3,2,1,0:T(8,128)(2,1)} %grads_hbm.1, f32[2,80,640]{2,1,0:T(8,128)} %moment_hbm.3), custom_call_target="tpu_custom_call" | custom-call | tf_op jit(solution)/shard_map/pallas_call | solution.py:374
  73.4 2.1 %shard_map.42 = (bf16[2,80,5120]{2,1,0:T(8,128)(2,1)}, f32[2,80,640]{2,1,0:T(8,128)}) custom-call(bf16[2,80,5120]{2,1,0:T(8,128)(2,1)S(1)} %get-tuple-element.5.gathered, f32[80,80]{1,0:T(8,128)S(1)} %get-tuple-element.6.mix, bf16[1,80,5120]{2,1,0:T(8,128)(2,1)S(1)} %get-tuple-element.7.done, f32[2,80,640]{2,1,0:T(8,128)} %moment_hbm.3), custom_call_target="tpu_custom_call" | custom-call | tf_op jit(solution)/shard_map/pallas_call | solution.py:406

commit v5 on v4

--- a/solution.py
+++ b/solution.py
@@ -24,10 +24,9 @@
 EARLY = 4
 PIECES = 4
 GROUP = 4
-LAG_MIDDLE = 5
 BURST = 4
 SETTLE = 14
-LAG = 5
+LAGS = (35, 23, 14, 5)
 
 
 def rates(n):
@@ -36,7 +35,7 @@
 
 
 def kernel(
-    n, axes, grads_hbm, moment_hbm, gathered, mix_out, done_out,
+    n, axes, grads_hbm, moment_hbm, gathered, mix_out, done_out, fresh,
     grads, moment, inward_part, cross_part, gram, squares, plane_in, ring_in,
     load_sem, inward_recv, cross_recv, outward_recv, inward_send, outward_send,
     plane_send, plane_recv, ring_send, ring_recv,
@@ -184,7 +183,9 @@
     def _():
         pl.semaphore_wait(barrier, 2 + len(offsets) + (halves - 1) * (n // 2))
 
-    wait_for = (2 * middle + 1 - 2 * depth) * LAG - lax.div(depth, middle) * (LAG - LAG_MIDDLE)
+    wait_for = (
+        LAGS[0] + lax.div(depth + 2, 3) * (LAGS[1] - LAGS[0]) + lax.div(depth, 2) * (LAGS[2] - LAGS[1])
+        + lax.div(depth, 3) * (LAGS[3] - LAGS[2]))
 
     def plane_copy(k, offset):
         return pltpu.make_async_remote_copy(
@@ -206,7 +207,7 @@
         for at in range(plane - 1):
             total = total + plane_in[k, at]
         squares[1, k] = total
-        for offset in range(1, reach):
+        for offset in reversed(range(1, reach)):
             ring_copy(k, offset).start()
 
     def norm_factor(k):
@@ -270,7 +271,7 @@
 
     @pl.when(depth == middle)
     def _():
-        for offset in offsets:
+        for offset in sorted(offsets, key=lambda o: -links_away(o, axes)):
             plane_copy(final, offset).start()
 
     early = []
@@ -284,6 +285,10 @@
 
     for k in range(final):
         apply_mix(early[k], gathered, k, lambda window, value: done_out.__setitem__((k, slice(None), window), value))
+
+    for k in range(layers):
+        average = (gathered[k, :, mine].astype(jnp.float32) - mixed * moment[k]) / n
+        fresh[k] = MOMENTUM_RATE * moment[k] + average
 
     trace = jnp.sum(gram[final] * eye, axis=(0, 1), keepdims=True) + TINY
     one = gram[final] / trace
@@ -318,6 +323,12 @@
                 ring_copy(k, offset).wait_send()
 
 
+def links_away(offset, axes):
+    _, xs, ys, cores = axes
+    across_x, across_y = offset // (ys * cores), offset // cores % ys
+    return min(across_x, xs - across_x) + min(across_y, ys - across_y)
+
+
 def apply_mix(mix, gathered, k, put):
     rows, cols = gathered.shape[1:]
     high = mix.astype(jnp.bfloat16)
@@ -330,15 +341,15 @@
         put(window, (value[:rows] + value[rows:]).astype(jnp.bfloat16))
 
 
-def finish(n, gathered, mix, done, moment_hbm, out_hbm, next_hbm, moment, fresh, result, load_sem, store_sem):
+def finish(gathered, mix, done, fresh, out_hbm, next_hbm, result, store_sem):
     layers, rows, cols = gathered.shape
-    width = cols // n
     final = layers - 1
-    mixed = rates(n)[1]
-    load = pltpu.make_async_copy(moment_hbm, moment, load_sem)
-    load.start()
-    stores = [pltpu.make_async_copy(done, out_hbm.at[pl.ds(0, final)], store_sem.at[0])]
-    stores[-1].start()
+    stores = [
+        pltpu.make_async_copy(done, out_hbm.at[pl.ds(0, final)], store_sem.at[0]),
+        pltpu.make_async_copy(fresh, next_hbm, store_sem.at[1]),
+    ]
+    for store in stores:
+        store.start()
 
     def put(window, value):
         result[:, window] = value
@@ -348,13 +359,6 @@
         stores.append(store)
 
     apply_mix(mix[...], gathered, final, put)
-    load.wait()
-    mine = pl.ds(pl.multiple_of(lax.axis_index("replica") * width, LANES), width)
-    for k in range(layers):
-        average = (gathered[k, :, mine].astype(jnp.float32) - mixed * moment[k]) / n
-        fresh[k] = MOMENTUM_RATE * moment[k] + average
-        stores.append(pltpu.make_async_copy(fresh.at[k], next_hbm.at[k], store_sem.at[len(stores)]))
-        stores[-1].start()
     for store in stores:
         store.wait()
 
@@ -370,16 +374,16 @@
     any_spec = pl.BlockSpec(memory_space=pl.ANY)
     vmem_spec = pl.BlockSpec(memory_space=pltpu.VMEM)
     bf16, f32 = jnp.bfloat16, jnp.float32
-    momentum = pltpu.with_memory_space_constraint(momentum, pltpu.HBM)
-    gathered, mix, done = pl.pallas_call(
+    gathered, mix, done, fresh = pl.pallas_call(
         functools.partial(kernel, n, axes),
         out_shape=(
             jax.ShapeDtypeStruct((layers, rows, cols), bf16),
             jax.ShapeDtypeStruct((rows, rows), f32),
             jax.ShapeDtypeStruct((layers - 1, rows, cols), bf16),
+            jax.ShapeDtypeStruct((layers, rows, width), f32),
         ),
         in_specs=[any_spec, any_spec],
-        out_specs=(vmem_spec, vmem_spec, vmem_spec),
+        out_specs=(vmem_spec, vmem_spec, vmem_spec, vmem_spec),
         scratch_shapes=[
             pltpu.VMEM((layers, rows, cols), bf16),
             pltpu.VMEM((layers, rows, width), f32),
@@ -402,24 +406,22 @@
         ],
         compiler_params=pltpu.CompilerParams(
             collective_id=0, has_side_effects=True, vmem_limit_bytes=40 * 1024 * 1024),
-    )(pltpu.with_memory_space_constraint(pseudo_grads, pltpu.HBM), momentum)
+    )(pltpu.with_memory_space_constraint(pseudo_grads, pltpu.HBM),
+      pltpu.with_memory_space_constraint(momentum, pltpu.HBM))
     return pl.pallas_call(
-        functools.partial(finish, n),
+        finish,
         out_shape=(
             jax.ShapeDtypeStruct((layers, rows, cols), bf16),
             jax.ShapeDtypeStruct((layers, rows, width), f32),
         ),
-        in_specs=[vmem_spec, vmem_spec, vmem_spec, any_spec],
+        in_specs=[vmem_spec, vmem_spec, vmem_spec, vmem_spec],
         out_specs=(any_spec, any_spec),
         scratch_shapes=[
-            pltpu.VMEM((layers, rows, width), f32),
-            pltpu.VMEM((layers, rows, width), f32),
             pltpu.VMEM((rows, cols), bf16),
-            dma,
-            dma((1 + layers + PIECES,)),
+            dma((2 + PIECES,)),
         ],
         compiler_params=pltpu.CompilerParams(vmem_limit_bytes=40 * 1024 * 1024),
-    )(gathered, mix, done, momentum)
+    )(gathered, mix, done, fresh)
 
 
 def solution(mesh, axes=SHARD_AXES):

time: 75.7 us -> 74.8 us (0.988)
  Pallas kernels: 74.9 us -> 74 us
    pallas_call x1, Pallas kernels: 2.13 us -> 1.34 us  [body(): pl.pallas_call(finish, out_shape=(jax.ShapeDtypeStruct((layers, rows, col...]
where the time goes in v5:
time: 74.8 us; the launch traced here: 74.6 us
  Pallas kernels  74 us (99%)
    pallas_call x1, Pallas kernels, body(): pl.pallas_call(functools.partial(kernel, n, axes), out_shape=(jax.ShapeDt...  72.6 us

profile of v5, /device:TPU:1, one launch (start us, length us, event | category | flops | bytes accessed | tf_op | source)
XLA Modules:
  0.0 74.6 jit_solution(253441501157027909)
XLA Ops:
  0.6 72.6 %shard_map.41 = (bf16[2,80,5120]{2,1,0:T(8,128)(2,1)S(1)}, f32[80,80]{1,0:T(8,128)S(1)}, bf16[1,80,5120]{2,1,0:T(8,128)(2,1)S(1)}, f32[2,80,640]{2,1,0:T(8,128)S(1)}) custom-call(bf16[1,2,80,5120]{3,2,1,0:T(8,128)(2,1)} %grads_hbm.1, f32[2,80,640]{2,1,0:T(8,128)} %moment_hbm.1), custom_call_target="tpu_custom_call" | custom-call | tf_op jit(solution)/shard_map/pallas_call | solution.py:377
  73.3 1.3 %shard_map.42 = (bf16[2,80,5120]{2,1,0:T(8,128)(2,1)}, f32[2,80,640]{2,1,0:T(8,128)}) custom-call(bf16[2,80,5120]{2,1,0:T(8,128)(2,1)S(1)} %get-tuple-element.6.gathered, f32[80,80]{1,0:T(8,128)S(1)} %get-tuple-element.7.mix, bf16[1,80,5120]{2,1,0:T(8,128)(2,1)S(1)} %get-tuple-element.8.done, f32[2,80,640]{2,1,0:T(8,128)S(1)} %get-tuple-element.9.fresh), custom_call_target="tpu_custom_call" | custom-call | tf_op jit(solution)/shard_map/pallas_call | solution.py:411

commit v6 on v5

--- a/solution.py
+++ b/solution.py
@@ -15,7 +15,6 @@
 MOMENTUM_RATE = 0.9
 EPSILON = 1e-07
 TINY = 1e-30
-EXACTNESS = lax.Precision.HIGHEST
 MESH = pl.DeviceIdType.MESH
 
 SHARD_AXES = (2, 4, 4, 2)
@@ -26,6 +25,7 @@
 GROUP = 4
 BURST = 4
 SETTLE = 14
+HEADROOM = 6
 LAGS = (35, 23, 14, 5)
 
 
@@ -227,34 +227,17 @@
         norm = gain * jnp.sqrt(jnp.sum(total, axis=1, keepdims=True))
         return gain / (norm + EPSILON)
 
-    def step(t, carry):
-        @pl.when(t < messages)
-        def _():
-            send_inward(t)
-
-        @pl.when(t >= wait_for)
-        def _():
-            send_outward(t - wait_for)
-
-        for k in range(layers - 1):
-            since = t - wait_for - (k + 1) * per_layer
-
-            for q in range(BURST):
-                @pl.when((depth == middle) & (since >= 0) & (since * BURST + q + 1 < plane))
-                def _():
-                    plane_copy(k, since * BURST + q + 1).start()
-
-            @pl.when((depth == middle) & (since == SETTLE))
-            def _():
-                plane_sum(k)
-
-        return carry
-
-    lax.fori_loop(0, messages + wait_for, step, 0)
-
     eye = (lax.broadcasted_iota(jnp.int32, (rows, rows), 0) == lax.broadcasted_iota(jnp.int32, (rows, rows), 1))
     eye = eye.astype(jnp.float32)
-    product = functools.partial(jnp.dot, precision=EXACTNESS, preferred_element_type=jnp.float32)
+    def split(value):
+        high = value.astype(jnp.bfloat16)
+        return high, (value - high.astype(jnp.float32)).astype(jnp.bfloat16)
+
+    def product(a, b):
+        dot = functools.partial(jnp.dot, preferred_element_type=jnp.float32)
+        (a_high, a_low), (b_high, b_low) = split(a), split(b)
+        return dot(a_high, b_high) + (dot(a_high, b_low) + dot(a_low, b_high))
+
 
     def polynomial(state, square):
         return QUINTIC_FIRST * eye + QUINTIC_SECOND * state + QUINTIC_THIRD * square
@@ -269,22 +252,52 @@
 
     final = layers - 1
 
+    def early_layers():
+        for k in range(final):
+            factor = norm_factor(k)
+            mix = newton_schulz(gram[k] * (factor * factor), None, ITERS) * (factor * math.sqrt(cols))
+            apply_mix(mix, gathered, k, lambda window, value: done_out.__setitem__((k, slice(None), window), value))
+
+    steps = messages + wait_for
+    early_at = steps - (1 - lax.div(depth + 2, 3)) * HEADROOM
+
+    def step(t, carry):
+        @pl.when(t < messages)
+        def _():
+            send_inward(t)
+
+        @pl.when((t >= wait_for) & (t < steps))
+        def _():
+            send_outward(t - wait_for)
+
+        for k in range(layers - 1):
+            since = t - wait_for - (k + 1) * per_layer
+
+            for q in range(BURST):
+                @pl.when((depth == middle) & (since >= 0) & (since * BURST + q + 1 < plane))
+                def _():
+                    plane_copy(k, since * BURST + q + 1).start()
+
+            @pl.when((depth == middle) & (since == SETTLE))
+            def _():
+                plane_sum(k)
+
+        @pl.when((depth == middle) & (t == steps))
+        def _():
+            for offset in sorted(offsets, key=lambda o: -links_away(o, axes)):
+                plane_copy(final, offset).start()
+
+        @pl.when(t == early_at)
+        def _():
+            early_layers()
+
+        return carry
+
+    lax.fori_loop(0, steps + 1, step, 0)
+
     @pl.when(depth == middle)
     def _():
-        for offset in sorted(offsets, key=lambda o: -links_away(o, axes)):
-            plane_copy(final, offset).start()
-
-    early = []
-    for k in range(final):
-        factor = norm_factor(k)
-        early.append(newton_schulz(gram[k] * (factor * factor), None, ITERS) * (factor * math.sqrt(cols)))
-
-    @pl.when(depth == middle)
-    def _():
         plane_sum(final)
-
-    for k in range(final):
-        apply_mix(early[k], gathered, k, lambda window, value: done_out.__setitem__((k, slice(None), window), value))
 
     for k in range(layers):
         average = (gathered[k, :, mine].astype(jnp.float32) - mixed * moment[k]) / n

time: 74.8 us -> 74.8 us (level)
  no operation moved by 1% of the time
where the time goes in v6:
time: 74.8 us; the launch traced here: 74.6 us
  Pallas kernels  74 us (99%)
    pallas_call x1, Pallas kernels, body(): pl.pallas_call(functools.partial(kernel, n, axes), out_shape=(jax.ShapeDt...  72.6 us

profile of v6, /device:TPU:1, one launch (start us, length us, event | category | flops | bytes accessed | tf_op | source)
XLA Modules:
  0.0 74.6 jit_solution(4798577219247592946)
XLA Ops:
  0.6 72.6 %shard_map.41 = (bf16[2,80,5120]{2,1,0:T(8,128)(2,1)S(1)}, f32[80,80]{1,0:T(8,128)S(1)}, bf16[1,80,5120]{2,1,0:T(8,128)(2,1)S(1)}, f32[2,80,640]{2,1,0:T(8,128)S(1)}) custom-call(bf16[1,2,80,5120]{3,2,1,0:T(8,128)(2,1)} %grads_hbm.1, f32[2,80,640]{2,1,0:T(8,128)} %moment_hbm.1), custom_call_target="tpu_custom_call" | custom-call | tf_op jit(solution)/shard_map/pallas_call | solution.py:390
  73.3 1.3 %shard_map.42 = (bf16[2,80,5120]{2,1,0:T(8,128)(2,1)}, f32[2,80,640]{2,1,0:T(8,128)}) custom-call(bf16[2,80,5120]{2,1,0:T(8,128)(2,1)S(1)} %get-tuple-element.6.gathered, f32[80,80]{1,0:T(8,128)S(1)} %get-tuple-element.7.mix, bf16[1,80,5120]{2,1,0:T(8,128)(2,1)S(1)} %get-tuple-element.8.done, f32[2,80,640]{2,1,0:T(8,128)S(1)} %get-tuple-element.9.fresh), custom_call_target="tpu_custom_call" | custom-call | tf_op jit(solution)/shard_map/pallas_call | solution.py:424
